TPU v7x, 512 devices: a whole 4x4x16 slice. The times are simulated.
512 devices in a mesh: wide: 64 (over z, x), narrow: 8 (over y, core).
Axes of the slice: x: 4, y: 4, z: 16, core: 2. Of those that a mesh axis runs over, the one named last changes fastest.
Arguments:
- hidden: bfloat16 [2048, 8192], P('wide', 'narrow'), may hold values from -6 to 6
- norm_gain: float32 [8192], P('narrow'), may hold values from 0.1 to 1.9
- head_weight: bfloat16 [8192, 32000], P('narrow', 'wide'), may hold values from -0.24 to 0.24
- diff_rows: bfloat16 [64, 8, 8, 32000], P('wide', 'narrow'), may hold values from -6 to 480
- slot_request: int32 [64, 8, 8], replicated, may hold values from 0 to 2047, as said below
- slot_code: int32 [64, 8, 8], replicated, may hold values from 1 to 8
- slot_count: int32 [64, 8], replicated, may hold values from 1 to 8, as said below
Outputs:
- log_probs: float32 [2048, 32000], P('narrow', 'wide')
Inputs may be any that keep to these rules, and one draw needn't show every extreme that they name: `slot_request`: within one pair, every request is named at most once. `slot_count`: slots at or beyond the count hold no row to use; in every draw some device uses all 8 slots.
All inputs are finite; a program needn't handle non-finite values.
Results may differ from a plain program's by a relative error of at most 0.0003.
Values may be sent and summed in bfloat16 or wider, within the bound.
A program may use at most 64 MiB of HBM per device.

v0:
```python
import jax
import jax.numpy as jnp
from jax import lax
from jax.sharding import PartitionSpec as P

D = 8192


epsilon = 1e-05


def combined_all(part, axis, combine):
    gathered = jax.tree.map(lambda a: lax.all_gather(a, axis), part)

    def take(source):
        return jax.tree.map(lambda a: lax.dynamic_index_in_dim(a, source, 0, False), gathered)

    return lax.fori_loop(
        1, lax.axis_size(axis), lambda source, state: combine(state, take(source)), take(0)
    )


def merge_pair(earlier, later):
    row_peak = jnp.maximum(earlier[0], later[0])
    summed = earlier[1] * jnp.exp(earlier[0] - row_peak) + later[1] * jnp.exp(later[0] - row_peak)
    return (row_peak, summed)


def body(hidden, norm_gain, head_weight, diff_rows, slot_request, slot_code, slot_count):
    values = hidden.astype(jnp.float32)
    squares = lax.psum(jnp.sum(values * values, axis=1), "narrow")
    scales = lax.rsqrt(squares / D + epsilon)
    normed = (values * scales[:, None] * norm_gain[None, :]).astype(jnp.bfloat16)
    partial_value = jnp.dot(
        lax.all_gather(normed, "wide", axis=0, tiled=True),
        head_weight,
        preferred_element_type=jnp.float32,
    )
    row_block = diff_rows[0, 0]
    arrived = lax.all_to_all(row_block, "wide", split_axis=1, concat_axis=0, tiled=True)
    slot_total = row_block.shape[0]
    active = jnp.arange(slot_total, dtype=jnp.int32)[None, None, :] < slot_count[:, :, None]
    weights = jnp.where(active, slot_code, 0).astype(jnp.float32) * 0.25
    base_block = lax.psum_scatter(partial_value, "narrow", scatter_dimension=0, tiled=True)
    owner_slices = lax.all_gather(arrived, "narrow", axis=0, tiled=True)
    targets = jnp.transpose(slot_request, (1, 0, 2)).reshape(-1)
    factor_all = jnp.transpose(weights, (1, 0, 2)).reshape(-1)
    block_rows = base_block.shape[0]
    offsets = targets - lax.axis_index("narrow") * block_rows
    owned = (offsets >= 0) & (offsets < block_rows)
    factors = jnp.where(owned, factor_all, 0.0)
    target_rows = jnp.where(owned, offsets, 0)
    own_block = base_block.at[target_rows].add(owner_slices.astype(jnp.float32) * factors[:, None])
    local_peak = jnp.max(own_block, axis=1)
    local_mass = jnp.sum(jnp.exp(own_block - local_peak[:, None]), axis=1)
    row_peak, row_mass = combined_all((local_peak, local_mass), "wide", merge_pair)
    log_total = row_peak + jnp.log(row_mass)
    return own_block - log_total[:, None]


def solution(mesh):
    placed = (
        P("wide", "narrow"),
        P("narrow"),
        P("narrow", "wide"),
        P("wide", "narrow", None, None),
        P(),
        P(),
        P(),
    )
    return jax.shard_map(
        body, mesh=mesh, in_specs=placed, out_specs=P("narrow", "wide"), check_vma=False
    )
```

profile of v0, /device:TPU:32, one launch (start us, length us, event | category | flops | bytes accessed | tf_op | source)
XLA Modules:
  0.0 463.6 jit_solution(9681761703783635985)
XLA Ops:
  6.5 0.0 copy-start
  6.5 0.0 all-gather.7.cloned.1.call-start
  6.5 1.0 fusion.4
  7.6 14.9 %psum.7 = f32[32]{0:T(128)S(1)} all-reduce(f32[32]{0:T(128)S(1)} %fusion.4), channel_id=1, replica_groups=mesh['wide'=64,'narrow'=8] {'narrow'}, use_global_device_ids=true, to_apply=%region_1.0 | all-reduce | flops 32 | bytes 256 | tf_op jit(solution)/shard_map/psum | solution.py:31
  22.5 1.6 fusion.6
  24.0 0.0 all-gather.7.cloned.1.call-update
  24.0 0.0 reduce-scatter.2.cloned.1.call-start
  24.1 147.9 %all-gather.7.cloned.1.call-done = bf16[2048,1024]{1,0:T(8,128)(2,1)} async-done(((bf16[32,1024]{1,0:T(8,128)(2,1)}), bf16[2048,1024]{1,0:T(8,128)(2,1)}) %all-gather.7.cloned.1.call-update) | async-done | bytes 4194320 | tf_op jit(solution)/shard_map/all_gather | solution.py:35
  172.0 0.0 copy-done
  172.0 6.5 %fusion.7 = f32[2048,500]{0,1:T(8,128)} fusion(bf16[2048,1024]{1,0:T(8,128)(2,1)} %all-gather.7.cloned.1.call-done, bf16[1024,500]{0,1:T(8,128)(2,1)S(1)} %copy-done), kind=kOutput, calls=%fused_computation.24 | convolution fusion | flops 2097152000 | bytes 9314304 | tf_op jit(solution)/shard_map/dot_general | solution.py:34
  178.5 0.0 reduce-scatter.2.cloned.1.call-update
  178.5 0.0 all-gather.9.cloned.1.call-start
  178.6 1.0 copy-done.1
  179.5 1.1 all_to_all.14
  180.7 0.3 copy.20
  181.0 32.8 %all_to_all.19 = bf16[8,64,500]{2,0,1:T(8,128)(2,1)} all-to-all(bf16[8,64,500]{2,0,1:T(8,128)(2,1)S(1)} %copy.20), channel_id=1, replica_groups=mesh['wide'=64,'narrow'=8] {'wide'}, dimensions={1} | all-to-all | bytes 1024000 | tf_op jit(solution)/shard_map/all_to_all | solution.py:40
  213.8 0.0 all-gather.9.cloned.1.call-update
  213.8 0.1 copy.19
  214.0 0.2 sub.63
  214.2 0.1 copy.21
  214.3 0.2 select_n.54
  214.5 5.4 %reduce-scatter.2.cloned.1.call-done = f32[256,500]{0,1:T(8,128)} async-done(((f32[2048,500]{0,1:T(8,128)}), f32[256,500]{0,1:T(8,128)}) %reduce-scatter.2.cloned.1.call-update) | async-done | bytes 512016 | tf_op jit(solution)/shard_map/reduce_scatter | solution.py:44
  219.9 1.2 copy.22
  221.1 39.4 %all-gather.9.cloned.1.call-done = bf16[4096,500]{1,0:T(8,128)(2,1)} async-done(((bf16[512,500]{1,0:T(8,128)(2,1)}), bf16[4096,500]{1,0:T(8,128)(2,1)}) %all-gather.9.cloned.1.call-update) | async-done | bytes 4096016 | tf_op jit(solution)/shard_map/all_gather | solution.py:45
  260.5 28.7 %scatter_custom_fusion = f32[256,500]{1,0:T(8,128)S(1)} fusion(f32[256,500]{1,0:T(8,128)S(1)} %copy.22, s32[4096]{0:T(1024)S(1)} %bitcast.35, bf16[4096,500]{1,0:T(8,128)(2,1)} %all-gather.9.cloned.1.call-done, f32[4096]{0:T(1024)S(1)} %select_n.54), kind=kCustom, calls=%fused_computation.4 | custom fusion | flops 6144000 | bytes 4624384 | tf_op jit(solution)/shard_map/scatter-add | solution.py:53
  289.1 0.2 copy.23
  289.3 0.1 reduce_max.9
  289.5 0.2 exponential_reduce_fusion
  289.7 82.5 %all-gather.2 = f32[64,1,256]{2,1,0:T(1,128)S(1)} all-gather(f32[1,1,256]{2,1,0:T(1,128)S(1)} %bitcast.36), channel_id=2, replica_groups=mesh['wide'=64,'narrow'=8] {'wide'}, dimensions={0}, use_global_device_ids=true | all-gather | bytes 66560 | tf_op jit(solution)/shard_map/all_gather | solution.py:13
  372.2 80.4 %all-gather.3 = f32[64,1,256]{2,1,0:T(1,128)S(1)} all-gather(f32[1,1,256]{2,1,0:T(1,128)S(1)} %bitcast.37), channel_id=3, replica_groups=mesh['wide'=64,'narrow'=8] {'wide'}, dimensions={0}, use_global_device_ids=true | all-gather | bytes 66560 | tf_op jit(solution)/shard_map/all_gather | solution.py:13
  452.6 3.6 while.17
  456.3 0.8 broadcast_subtract_fusion
  (142 shorter events, 2.1 us)
Async XLA Ops:
  6.5 165.5 %copy-start = (bf16[1024,500]{0,1:T(8,128)(2,1)S(1)}, bf16[1024,500]{0,1:T(8,128)(2,1)}, u32[]{:S(2)}) copy-start(bf16[1024,500]{0,1:T(8,128)(2,1)} %param.11) | copy-start | bytes 3072004
  6.5 165.5 %all-gather.7.cloned.1.call-start = ((), (), s32[]{:S(2)}) async-start(), calls=%async_computation.2 | async-start | bytes 4259840 | tf_op jit(solution)/shard_map/all_gather | solution.py:35
  24.0 195.8 %reduce-scatter.2.cloned.1.call-start = ((), (), s32[]{:S(2)}) async-start(), calls=%async_computation.3 | async-start | bytes 4644864 | tf_op jit(solution)/shard_map/reduce_scatter | solution.py:44
  178.5 1.0 copy-start.1
  178.5 35.3 %copy-start.2 = (s32[64,8,8]{0,2,1:T(8,128)S(1)}, s32[64,8,8]{0,2,1:T(8,128)}, u32[]{:S(2)}) copy-start(s32[64,8,8]{0,2,1:T(8,128)} %param.13) | copy-start | bytes 49156
  178.5 35.7 %copy-start.3 = (s32[64,8,8]{0,2,1:T(8,128)S(1)}, s32[64,8,8]{0,2,1:T(8,128)}, u32[]{:S(2)}) copy-start(s32[64,8,8]{0,2,1:T(8,128)} %param.14) | copy-start | bytes 49156
  178.5 35.7 %copy-start.4 = (s32[64,8]{0,1:T(8,128)S(1)}, s32[64,8]{0,1:T(8,128)}, u32[]{:S(2)}) copy-start(s32[64,8]{0,1:T(8,128)} %param.15) | copy-start | bytes 6148
  178.5 82.0 %all-gather.9.cloned.1.call-start = ((), (), s32[]{:S(2)}) async-start(), calls=%async_computation.4 | async-start | bytes 4718592 | tf_op jit(solution)/shard_map/all_gather | solution.py:45
Sparse Core Ops, SparseCore 0:
  24.2 147.8 all-gather.6
  178.6 41.1 reduce-scatter.1
  222.3 38.1 all-gather.8
where the time goes:
time: 464 us
  blocking collectives  211 us (45%)
  waiting for transfers between devices  193 us (42%)
  other arithmetic  33.8 us (7%)
  between operations  13.3 us (3%)
  matrix products  6.47 us (1%)
  local copies, waits for them, and re-layouts  5.1 us (1%)
    all_gather x2, blocking collectives, combined_all(): gathered = jax.tree.map(lambda a: lax.all_gather(a, axis), part)  163 us
    all_gather x1, waiting for transfers between devices, body(): lax.all_gather(normed, 'wide', axis=0, tiled=True)  148 us
    all_gather x1, waiting for transfers between devices, body(): owner_slices = lax.all_gather(arrived, 'narrow', axis=0, tiled=True)  39.4 us
    all_to_all x1, blocking collectives, body(): lax.all_to_all(row_block, 'wide', split_axis=1, concat_axis=0, tiled=True)  32.8 us
    scatter-add x1, other arithmetic, body(): base_block.at[target_rows]  28.7 us
    psum x1, blocking collectives, body(): squares = lax.psum(jnp.sum(values * values, axis=1), 'narrow')  14.9 us
  transfers between devices with their start and end apart: 3, of which 3 were waited for; matrix products, arithmetic and copies ran while one was open for 0% of the time, Pallas kernels for 0%

commit v1 on v0

v1 whole, which is shorter than its diff:
```python
import functools

import jax
import jax.numpy as jnp
from jax import lax
from jax.experimental import pallas as pl
from jax.experimental.pallas import tpu as pltpu
from jax.sharding import PartitionSpec as P

D = 8192
EPS = 1e-05
NZ, NX, NY, NC = 16, 4, 4, 2
NW, NN = NZ * NX, NY * NC
REQ = 32
ROWS = 256
VOC = 500
PADV = 512
CAP = 8
SLOTS = NW * CAP

f32 = jnp.float32
bf16 = jnp.bfloat16
NT = (((1,), (1,)), ((), ()))


def remote(src, dst, send, recv, wide, narrow):
    return pltpu.make_async_remote_copy(
        src_ref=src,
        dst_ref=dst,
        send_sem=send,
        recv_sem=recv,
        device_id={"wide": wide, "narrow": narrow},
        device_id_type=pl.DeviceIdType.MESH,
    )


def head_kernel(
    h_ref, g_ref, wt_ref, rows_ref, code_ref, o_ref,
    act, recv_rows, rows_t, part, pair, half, full, sq, peaks_x, peaks_z,
    sq_send, sq_recv, a2a_send, a2a_recv, z_send, z_recv, x_send, x_recv, h_send, h_recv,
    p_send, p_recv, y_send, y_recv, sx_send, sx_recv, sz_send, sz_recv,
):
    w = lax.axis_index("wide")
    n = lax.axis_index("narrow")
    z, x, y, c = w // NX, w % NX, n // NC, n % NC

    def wide_of(dz, dx):
        return ((z + dz + NZ) % NZ) * NX + (x + dx + NX) % NX

    values = h_ref[...].astype(f32)
    sq[n] = jnp.broadcast_to(jnp.sum(values * values, axis=1, keepdims=True), (REQ, 128))

    def sq_copy(k):
        return remote(sq.at[n], sq.at[n], sq_send.at[k], sq_recv.at[k], w, (n + k) % NN)

    def sq_arrival(k):
        peer = (n - k + NN) % NN
        return remote(sq.at[peer], sq.at[peer], sq_send.at[k], sq_recv.at[k], w, peer)

    for k in range(1, NN):
        sq_copy(k).start()

    def a2a_copy(k):
        target = (w + k) % NW
        return remote(rows_ref.at[target], recv_rows.at[w], a2a_send, a2a_recv, target, n)

    def a2a_some(first, last):
        @pl.loop(first, last)
        def _(k):
            a2a_copy(k).start()

    a2a_some(1, 8)
    recv_rows[w] = rows_ref[w]

    for k in range(1, NN):
        sq_arrival(k).wait_recv()
    total = jnp.sum(sq[...], axis=0)[:, :1]
    scales = lax.rsqrt(total / D + EPS)
    act[w] = (values * scales * g_ref[...]).astype(bf16)

    top, bottom = pl.ds(0, REQ // 2), pl.ds(REQ // 2, REQ // 2)

    def z_copy(side, d, rows=None):
        step = 1 if side == 0 else -1
        block = act.at[wide_of(-step * d, 0)]
        block = block if rows is None else block.at[rows]
        return remote(block, block, z_send, z_recv.at[side, d + 1], wide_of(step, 0), n)

    def z_arrival(side, d, rows=None):
        step = 1 if side == 0 else -1
        block = act.at[wide_of(-step * d, 0)]
        block = block if rows is None else block.at[rows]
        return remote(block, block, z_send, z_recv.at[side, d], wide_of(step, 0), n)

    def x_copy(side, q, dz):
        step = 1 if side == 0 else -1
        block = act.at[wide_of(dz, 0)]
        return remote(block, block, x_send, x_recv.at[side, q], wide_of(0, step), n)

    def x_arrival(side, q, dz):
        step = 1 if side == 0 else -1
        block = act.at[wide_of(dz, -step)]
        return remote(block, block, x_send, x_recv.at[side, q], wide_of(0, step), n)

    def h_copy(side, q, dz):
        step = 1 if side == 0 else -1
        block = act.at[wide_of(dz, -step)].at[top if side == 0 else bottom]
        return remote(block, block, h_send, h_recv.at[side, q], wide_of(0, step), n)

    def h_arrival(side, q, dz):
        step = 1 if side == 0 else -1
        block = act.at[wide_of(dz, 2)].at[top if side == 0 else bottom]
        return remote(block, block, h_send, h_recv.at[side, q], wide_of(0, step), n)

    events = [[(0, 0)]] + [[(2 * d - 1, -d), (2 * d, d)] for d in range(1, 8)] + [[(15, 8)]]

    def forward_x(d):
        for q, dz in events[d]:
            for side in range(2):
                x_arrival(side, q, dz).wait_recv()
                h_copy(side, q, dz).start()

    LAG = 1
    for d in range(9):
        if d in range(1, 8):
            for side in range(2):
                z_arrival(side, d).wait_recv()
        if d == 8:
            z_arrival(0, 8, top).wait_recv()
            z_arrival(1, 8, bottom).wait_recv()
        if d < 7:
            for side in range(2):
                z_copy(side, d).start()
        if d == 7:
            z_copy(0, 7, top).start()
            z_copy(1, 7, bottom).start()
        for q, dz in events[d]:
            for side in range(2):
                x_copy(side, q, dz).start()
        if d < 8:
            a2a_some(8 + 7 * d, 15 + 7 * d)
        if d >= LAG:
            forward_x(d - LAG)
    for d in range(9 - LAG, 9):
        forward_x(d)
    for d in range(9):
        for q, dz in events[d]:
            for side in range(2):
                h_arrival(side, q, dz).wait_recv()

    pltpu.make_async_copy(rows_ref.at[pl.ds(0, NW - 1)], recv_rows.at[pl.ds(0, NW - 1)], a2a_recv).wait()
    rows_t[...] = jnp.transpose(recv_rows[...].reshape(SLOTS, PADV))

    code = code_ref[...]
    requests = code // 16
    quarters = (code % 16).astype(f32) * 0.25

    def product(block):
        requested = lax.broadcasted_iota(jnp.int32, (ROWS, SLOTS), 0) + block * ROWS
        chosen = jnp.where(requests == requested, quarters, 0.0).astype(bf16)
        left = act[pl.ds(block * (ROWS // REQ), ROWS // REQ)].reshape(ROWS, D // NN)
        part[block] = lax.dot_general(wt_ref[...], left, NT, preferred_element_type=f32) + lax.dot_general(
            rows_t[pl.ds(0, VOC)], chosen, NT, preferred_element_type=f32
        )

    def mine(r):
        return ((y + r) % NY) * NC + c

    def theirs(r):
        return ((y + r) % NY) * NC + 1 - c

    def pair_copy(r):
        return remote(part.at[theirs(r)], pair.at[r], p_send.at[r], p_recv.at[r], w, y * NC + 1 - c)

    def north(k):
        return ((y + k + NY) % NY) * NC + c

    lanes = (pl.ds(0, ROWS // 2), pl.ds(ROWS // 2, ROWS // 2))

    def half_copy(side):
        step = 1 if side == 0 else -1
        return remote(
            part.at[mine(2)].at[:, lanes[side]], half.at[side], y_send.at[side], y_recv.at[side], w, north(step)
        )

    def full_copy(side):
        step = 1 if side == 0 else -1
        return remote(part.at[mine(step % NY)], full.at[side], y_send.at[2 + side], y_recv.at[2 + side], w, north(step))

    order = (2, 1, 3, 0)
    for r in order:
        product(theirs(r))
        pair_copy(r).start()
    for r in order:
        block = mine(r)
        product(block)
        pair_copy(r).wait_recv()
        part[block] += pair[r]
        if r == 2:
            half_copy(0).start()
            half_copy(1).start()
    for side in range(2):
        block = mine(1 if side == 0 else 3)
        half_copy(side).wait_recv()
        part[block, :, lanes[side]] += half[side]
        full_copy(side).start()
    for side in range(2):
        full_copy(side).wait_recv()
    logits = part[mine(0)] + full[0] + full[1]

    def merged(buffer):
        peaks, masses = buffer[:, 0:1, :], buffer[:, 4:5, :]
        peak = jnp.max(peaks, axis=0)
        return peak, jnp.sum(masses * jnp.exp(peaks - peak[None]), axis=0)

    def put(buffer, index, peak, mass):
        buffer[index, 0:4, :] = jnp.broadcast_to(peak, (4, ROWS))
        buffer[index, 4:8, :] = jnp.broadcast_to(mass, (4, ROWS))

    peak = jnp.max(logits, axis=0, keepdims=True)
    mass = jnp.sum(jnp.exp(logits - peak), axis=0, keepdims=True)
    put(peaks_x, x, peak, mass)

    def sx_copy(k):
        return remote(peaks_x.at[x], peaks_x.at[x], sx_send.at[k], sx_recv.at[k], wide_of(0, k), n)

    for k in range(1, NX):
        sx_copy(k).start()
    for k in range(1, NX):
        sx_copy(k).wait_recv()
    peak, mass = merged(peaks_x)
    put(peaks_z, z, peak, mass)

    def sz_copy(k):
        return remote(peaks_z.at[z], peaks_z.at[z], sz_send.at[k], sz_recv.at[k], wide_of(k, 0), n)

    for k in range(1, NZ):
        sz_copy(k).start()
    for k in range(1, NZ):
        sz_copy(k).wait_recv()
    peak, mass = merged(peaks_z)
    o_ref[...] = logits - (peak + jnp.log(mass))

    for k in range(1, NN):
        sq_copy(k).wait_send()
    pltpu.make_async_copy(rows_ref.at[pl.ds(0, NW - 1)], recv_rows.at[pl.ds(0, NW - 1)], a2a_send).wait()
    pltpu.make_async_copy(act.at[pl.ds(0, 15)], act.at[pl.ds(0, 15)], z_send).wait()
    pltpu.make_async_copy(act.at[pl.ds(0, 32)], act.at[pl.ds(0, 32)], x_send).wait()
    pltpu.make_async_copy(act.at[pl.ds(0, 16)], act.at[pl.ds(0, 16)], h_send).wait()
    for r in range(NY):
        pair_copy(r).wait_send()
    for side in range(2):
        half_copy(side).wait_send()
        full_copy(side).wait_send()
    for k in range(1, NX):
        sx_copy(k).wait_send()
    for k in range(1, NZ):
        sz_copy(k).wait_send()


def body(hidden, norm_gain, head_weight, diff_rows, slot_request, slot_code, slot_count):
    n = lax.axis_index("narrow")
    rows = jnp.transpose(diff_rows[0, 0].reshape(CAP, NW, VOC), (1, 0, 2))
    rows = jnp.pad(rows, ((0, 0), (0, 0), (0, PADV - VOC)))
    live = jnp.arange(CAP, dtype=jnp.int32)[None, None, :] < slot_count[:, :, None]
    coded = slot_request * 16 + jnp.where(live, slot_code, 0)
    code = lax.dynamic_index_in_dim(coded, n, 1, False).reshape(1, SLOTS)
    dma = pltpu.SemaphoreType.DMA
    vmem = pl.BlockSpec(memory_space=pltpu.VMEM)
    out = pl.pallas_call(
        head_kernel,
        name="head",
        out_shape=jax.ShapeDtypeStruct((VOC, ROWS), f32),
        in_specs=[vmem] * 5,
        out_specs=vmem,
        scratch_shapes=[
            pltpu.VMEM((NW, REQ, D // NN), bf16),
            pltpu.VMEM((NW, CAP, PADV), bf16),
            pltpu.VMEM((PADV, SLOTS), bf16),
            pltpu.VMEM((NN, VOC, ROWS), f32),
            pltpu.VMEM((NY, VOC, ROWS), f32),
            pltpu.VMEM((2, VOC, ROWS // 2), f32),
            pltpu.VMEM((2, VOC, ROWS), f32),
            pltpu.VMEM((NN, REQ, 128), f32),
            pltpu.VMEM((NX, 8, ROWS), f32),
            pltpu.VMEM((NZ, 8, ROWS), f32),
            dma((NN,)), dma((NN,)), dma, dma, dma, dma((2, 9)), dma, dma((2, 16)), dma, dma((2, 16)),
            dma((NY,)), dma((NY,)), dma((4,)), dma((4,)), dma((NX,)), dma((NX,)), dma((NZ,)), dma((NZ,)),
        ],
        compiler_params=pltpu.CompilerParams(has_side_effects=True, vmem_limit_bytes=40 << 20),
    )(hidden, norm_gain[None, :], head_weight.T, rows, code)
    return out.T


def solution(mesh):
    placed = (
        P("wide", "narrow"),
        P("narrow"),
        P("narrow", "wide"),
        P("wide", "narrow", None, None),
        P(),
        P(),
        P(),
    )
    return jax.shard_map(
        body, mesh=mesh, in_specs=placed, out_specs=P("narrow", "wide"), check_vma=False
    )
```

time: 464 us -> 131 us (0.28)
  the two profiles are of different devices: /device:TPU:32 before, /device:TPU:8 now
where the time goes in v1:
time: 131 us; the launch traced here: 130 us
  Pallas kernels  126 us (96%)
  local copies, waits for them, and re-layouts  4.04 us (3%)
    pallas_call x1, Pallas kernels, body(): pl.pallas_call(head_kernel, name='head', out_shape=jax.ShapeDtypeStruct((...  126 us

profile of v1, /device:TPU:8, one launch (start us, length us, event | category | flops | bytes accessed | tf_op | source)
XLA Modules:
  0.0 130.4 jit_solution(9053984393565247221)
XLA Ops:
  0.0 0.0 copy-start
  0.0 2.1 %reshape_squeeze.3 = bf16[8,64,500]{2,1,0:T(8,128)(2,1)S(1)} reshape(bf16[1,1,8,32000]{3,2,1,0:T(8,128)(2,1)} %param.10) | data formatting | bytes 1024000 | tf_op jit(solution)/shard_map/reshape;squeeze | solution.py:263
  2.1 0.0 copy-start.1
  2.1 0.3 copy.12
  2.4 0.1 pad.4.rows_ref
  2.5 0.0 copy-start.2
  2.5 0.0 copy-done
  2.5 0.7 fusion
  3.3 0.1 copy.10
  3.3 0.0 copy-start.3
  3.3 0.1 reshape.5.code_ref
  3.4 0.0 copy-done.1
  3.4 0.0 copy-done.2
  3.5 0.6 copy-done.3
  4.0 125.6 %head.1 = f32[500,256]{1,0:T(8,128)S(1)} custom-call(bf16[32,1024]{1,0:T(8,128)(2,1)S(1)} %copy-done.2, f32[1,1024]{1,0:T(1,128)S(1)} %bitcast.12, bf16[500,1024]{1,0:T(8,128)(2,1)S(1)} %bitcast.11, bf16[64,8,512]{2,1,0:T(8,128)(2,1)S(1)} %pad.4.rows_ref, s32[1,512]{1,0:T(1,128)S(1)} %reshape.5.code_ref), custom_call_target="tpu_custom_call" | custom-call | tf_op jit(solution)/shard_map/head/pallas_call | solution.py:270
  129.7 0.8 copy.14
  (1 shorter events, 0.0 us)
Async XLA Ops:
  0.0 2.5 %copy-start = (s32[64,8]{0,1:T(8,128)S(1)}, s32[64,8]{0,1:T(8,128)}, u32[]{:S(2)}) copy-start(s32[64,8]{0,1:T(8,128)} %param.13) | copy-start | bytes 6148
  2.1 1.3 %copy-start.1 = (bf16[1024,500]{0,1:T(8,128)(2,1)S(1)}, bf16[1024,500]{0,1:T(8,128)(2,1)}, u32[]{:S(2)}) copy-start(bf16[1024,500]{0,1:T(8,128)(2,1)} %param.9) | copy-start | bytes 3072004
  2.5 0.9 copy-start.2
  3.3 0.7 copy-start.3

commit v2 on v1

--- a/solution.py
+++ b/solution.py
@@ -17,6 +17,7 @@
 PADV = 512
 CAP = 8
 SLOTS = NW * CAP
+FAR = (8, 7, 9, 6, 10, 5, 11, 4, 12, 3, 13, 2, 14, 1, 15)
 
 f32 = jnp.float32
 bf16 = jnp.bfloat16
@@ -35,9 +36,9 @@
 
 
 def head_kernel(
-    h_ref, g_ref, wt_ref, rows_ref, code_ref, o_ref,
-    act, recv_rows, rows_t, part, pair, half, full, sq, peaks_x, peaks_z,
-    sq_send, sq_recv, a2a_send, a2a_recv, z_send, z_recv, x_send, x_recv, h_send, h_recv,
+    h_ref, g_ref, wt_ref, diff_ref, req_ref, code_ref, count_ref, o_ref,
+    act, bundle, relay, recv_rows, rows_t, part, pair, half, full, sq, peaks_x, peaks_z,
+    sq_send, sq_recv, b_send, b_recv, a2a_send, a2a_recv, z_send, z_recv, x_send, x_recv, h_send, h_recv,
     p_send, p_recv, y_send, y_recv, sx_send, sx_recv, sz_send, sz_recv,
 ):
     w = lax.axis_index("wide")
@@ -47,8 +48,28 @@
     def wide_of(dz, dx):
         return ((z + dz + NZ) % NZ) * NX + (x + dx + NX) % NX
 
+    barrier = pltpu.get_barrier_semaphore()
+
+    def greet(wide, narrow):
+        pl.semaphore_signal(
+            barrier, inc=1, device_id={"wide": wide, "narrow": narrow}, device_id_type=pl.DeviceIdType.MESH
+        )
+
+    for k in range(1, NN):
+        greet(w, (n + k) % NN)
+    for k in range(1, NX):
+        greet(wide_of(0, k), n)
+    for k in range(1, NZ):
+        greet(wide_of(k, 0), n)
+
+    for target in range(NW):
+        bundle[target % NX, target // NX, :, 0:VOC] = diff_ref[:, target * VOC : (target + 1) * VOC]
+    relay[x] = bundle[x]
+
     values = h_ref[...].astype(f32)
     sq[n] = jnp.broadcast_to(jnp.sum(values * values, axis=1, keepdims=True), (REQ, 128))
+
+    pl.semaphore_wait(barrier, NN + NX + NZ - 3)
 
     def sq_copy(k):
         return remote(sq.at[n], sq.at[n], sq_send.at[k], sq_recv.at[k], w, (n + k) % NN)
@@ -60,17 +81,45 @@
     for k in range(1, NN):
         sq_copy(k).start()
 
-    def a2a_copy(k):
-        target = (w + k) % NW
-        return remote(rows_ref.at[target], recv_rows.at[w], a2a_send, a2a_recv, target, n)
-
-    def a2a_some(first, last):
-        @pl.loop(first, last)
-        def _(k):
-            a2a_copy(k).start()
-
-    a2a_some(1, 8)
-    recv_rows[w] = rows_ref[w]
+    def bundle_copy(k):
+        return remote(bundle.at[(x + k) % NX], relay.at[x], b_send.at[k], b_recv.at[k], wide_of(0, k), n)
+
+    def bundle_arrival(k):
+        peer = (x - k + NX) % NX
+        return remote(bundle.at[peer], relay.at[peer], b_send.at[k], b_recv.at[k], wide_of(0, k), n)
+
+    def relay_copy(source, k):
+        row = z * NX + source
+        return remote(
+            relay.at[source].at[(z + k) % NZ], recv_rows.at[row], a2a_send, a2a_recv, wide_of(k, 0), n
+        )
+
+    def relay_start(k):
+        source = (x - k + NX) % NX
+        recv_rows[z * NX + source] = relay[source, z]
+        for far in FAR:
+            relay_copy(source, far).start()
+
+    for k in (2, 1, 3):
+        bundle_copy(k).start()
+    relay_start(0)
+
+    live = lax.broadcasted_iota(jnp.int32, (CAP, NW), 0) < count_ref[pl.ds(n, 1), :]
+    code = jnp.where(live, code_ref[n], 0)
+    request = req_ref[n]
+    spread = (
+        lax.broadcasted_iota(jnp.int32, (NW, SLOTS), 1) // CAP == lax.broadcasted_iota(jnp.int32, (NW, SLOTS), 0)
+    ).astype(bf16)
+    picked = lax.broadcasted_iota(jnp.int32, (CAP, SLOTS), 1) % CAP == lax.broadcasted_iota(
+        jnp.int32, (CAP, SLOTS), 0
+    )
+
+    def as_row(small):
+        wide = jnp.dot(small.astype(f32).astype(bf16), spread, preferred_element_type=f32)
+        return jnp.sum(jnp.where(picked, wide, 0.0), axis=0, keepdims=True)
+
+    requests = as_row(request // 128) * 128.0 + as_row(request % 128)
+    quarters = as_row(code) * 0.25
 
     for k in range(1, NN):
         sq_arrival(k).wait_recv()
@@ -120,7 +169,27 @@
                 x_arrival(side, q, dz).wait_recv()
                 h_copy(side, q, dz).start()
 
-    LAG = 1
+    def last_x(d):
+        for q, dz in events[d]:
+            for side in range(2):
+                h_arrival(side, q, dz).wait_recv()
+
+    def block_of(d):
+        away = d // 2
+        sign = 1 if d % 2 else -1
+        return (z // 2 + jnp.where(z % 2 == 0, sign * away, -sign * away) + NN) % NN
+
+    def product(d):
+        block = block_of(d)
+        left = act[pl.ds(block * (ROWS // REQ), ROWS // REQ)].reshape(ROWS, D // NN)
+        part[block] = lax.dot_general(wt_ref[...], left, NT, preferred_element_type=f32)
+
+    def add_rows(d):
+        block = block_of(d)
+        requested = lax.broadcasted_iota(jnp.int32, (ROWS, SLOTS), 0) + block * ROWS
+        chosen = jnp.where(requests == requested.astype(f32), quarters, 0.0).astype(bf16)
+        part[block] += lax.dot_general(rows_t[pl.ds(0, VOC)], chosen, NT, preferred_element_type=f32)
+
     for d in range(9):
         if d in range(1, 8):
             for side in range(2):
@@ -137,76 +206,87 @@
         for q, dz in events[d]:
             for side in range(2):
                 x_copy(side, q, dz).start()
-        if d < 8:
-            a2a_some(8 + 7 * d, 15 + 7 * d)
-        if d >= LAG:
-            forward_x(d - LAG)
-    for d in range(9 - LAG, 9):
-        forward_x(d)
-    for d in range(9):
-        for q, dz in events[d]:
-            for side in range(2):
-                h_arrival(side, q, dz).wait_recv()
-
-    pltpu.make_async_copy(rows_ref.at[pl.ds(0, NW - 1)], recv_rows.at[pl.ds(0, NW - 1)], a2a_recv).wait()
+        if d < 3:
+            k = (1, 3, 2)[d]
+            bundle_arrival(k).wait_recv()
+            relay_start(k)
+        if d >= 1:
+            forward_x(d - 1)
+        if d >= 2:
+            last_x(d - 2)
+        if d >= 3:
+            product(d - 2)
+    forward_x(8)
+
+    pltpu.make_async_copy(recv_rows.at[pl.ds(0, 60)], recv_rows.at[pl.ds(0, 60)], a2a_recv).wait()
     rows_t[...] = jnp.transpose(recv_rows[...].reshape(SLOTS, PADV))
-
-    code = code_ref[...]
-    requests = code // 16
-    quarters = (code % 16).astype(f32) * 0.25
-
-    def product(block):
-        requested = lax.broadcasted_iota(jnp.int32, (ROWS, SLOTS), 0) + block * ROWS
-        chosen = jnp.where(requests == requested, quarters, 0.0).astype(bf16)
-        left = act[pl.ds(block * (ROWS // REQ), ROWS // REQ)].reshape(ROWS, D // NN)
-        part[block] = lax.dot_general(wt_ref[...], left, NT, preferred_element_type=f32) + lax.dot_general(
-            rows_t[pl.ds(0, VOC)], chosen, NT, preferred_element_type=f32
-        )
-
-    def mine(r):
-        return ((y + r) % NY) * NC + c
-
-    def theirs(r):
-        return ((y + r) % NY) * NC + 1 - c
-
-    def pair_copy(r):
-        return remote(part.at[theirs(r)], pair.at[r], p_send.at[r], p_recv.at[r], w, y * NC + 1 - c)
 
     def north(k):
         return ((y + k + NY) % NY) * NC + c
 
+    def away_of(block):
+        return (block // NC - y + NY) % NY
+
+    def pair_copy(block):
+        r = away_of(block)
+        return remote(part.at[block], pair.at[r], p_send.at[r], p_recv.at[r], w, y * NC + 1 - c)
+
     lanes = (pl.ds(0, ROWS // 2), pl.ds(ROWS // 2, ROWS // 2))
 
-    def half_copy(side):
-        step = 1 if side == 0 else -1
-        return remote(
-            part.at[mine(2)].at[:, lanes[side]], half.at[side], y_send.at[side], y_recv.at[side], w, north(step)
-        )
-
-    def full_copy(side):
-        step = 1 if side == 0 else -1
-        return remote(part.at[mine(step % NY)], full.at[side], y_send.at[2 + side], y_recv.at[2 + side], w, north(step))
-
-    order = (2, 1, 3, 0)
-    for r in order:
-        product(theirs(r))
-        pair_copy(r).start()
-    for r in order:
-        block = mine(r)
-        product(block)
-        pair_copy(r).wait_recv()
-        part[block] += pair[r]
-        if r == 2:
-            half_copy(0).start()
-            half_copy(1).start()
+    def half_copy(side, block):
+        step = 1 if side == 0 else -1
+        return remote(part.at[block].at[:, lanes[side]], half.at[side], y_send.at[side], y_recv.at[side], w, north(step))
+
+    def full_copy(side, block):
+        step = 1 if side == 0 else -1
+        return remote(part.at[block], full.at[side], y_send.at[2 + side], y_recv.at[2 + side], w, north(step))
+
+    def across_cores(d):
+        block = block_of(d)
+
+        @pl.when(block % NC != c)
+        def _():
+            pair_copy(block).start()
+
+    def from_core(d):
+        block = block_of(d)
+        r = away_of(block)
+
+        @pl.when(block % NC == c)
+        def _():
+            pair_copy(block).wait_recv()
+            part[block] += pair[r]
+
+        @pl.when((block % NC == c) & (r == 2))
+        def _():
+            half_copy(0, block).start()
+            half_copy(1, block).start()
+
+    def to_owner(d):
+        block = block_of(d)
+        r = away_of(block)
+        for side in range(2):
+
+            @pl.when((block % NC == c) & (r == (1, 3)[side]))
+            def _():
+                half_copy(side, block).wait_recv()
+                part[block, :, lanes[side]] += half[side]
+                full_copy(side, block).start()
+
+    for d in range(1, 17):
+        if d in (7, 8):
+            last_x(d)
+            product(d)
+        if d <= 8:
+            add_rows(d)
+            across_cores(d)
+        if 1 <= d - 3 <= 8:
+            from_core(d - 3)
+        if 1 <= d - 8 <= 8:
+            to_owner(d - 8)
     for side in range(2):
-        block = mine(1 if side == 0 else 3)
-        half_copy(side).wait_recv()
-        part[block, :, lanes[side]] += half[side]
-        full_copy(side).start()
-    for side in range(2):
-        full_copy(side).wait_recv()
-    logits = part[mine(0)] + full[0] + full[1]
+        full_copy(side, n).wait_recv()
+    logits = part[n] + full[0] + full[1]
 
     def merged(buffer):
         peaks, masses = buffer[:, 0:1, :], buffer[:, 4:5, :]
@@ -234,7 +314,7 @@
     def sz_copy(k):
         return remote(peaks_z.at[z], peaks_z.at[z], sz_send.at[k], sz_recv.at[k], wide_of(k, 0), n)
 
-    for k in range(1, NZ):
+    for k in FAR:
         sz_copy(k).start()
     for k in range(1, NZ):
         sz_copy(k).wait_recv()
@@ -243,15 +323,17 @@
 
     for k in range(1, NN):
         sq_copy(k).wait_send()
-    pltpu.make_async_copy(rows_ref.at[pl.ds(0, NW - 1)], recv_rows.at[pl.ds(0, NW - 1)], a2a_send).wait()
+    for k in range(1, NX):
+        bundle_copy(k).wait_send()
+    pltpu.make_async_copy(recv_rows.at[pl.ds(0, 60)], recv_rows.at[pl.ds(0, 60)], a2a_send).wait()
     pltpu.make_async_copy(act.at[pl.ds(0, 15)], act.at[pl.ds(0, 15)], z_send).wait()
     pltpu.make_async_copy(act.at[pl.ds(0, 32)], act.at[pl.ds(0, 32)], x_send).wait()
     pltpu.make_async_copy(act.at[pl.ds(0, 16)], act.at[pl.ds(0, 16)], h_send).wait()
     for r in range(NY):
-        pair_copy(r).wait_send()
+        pair_copy(((y + r) % NY) * NC + 1 - c).wait_send()
     for side in range(2):
-        half_copy(side).wait_send()
-        full_copy(side).wait_send()
+        half_copy(side, n).wait_send()
+        full_copy(side, n).wait_send()
     for k in range(1, NX):
         sx_copy(k).wait_send()
     for k in range(1, NZ):
@@ -259,22 +341,18 @@
 
 
 def body(hidden, norm_gain, head_weight, diff_rows, slot_request, slot_code, slot_count):
-    n = lax.axis_index("narrow")
-    rows = jnp.transpose(diff_rows[0, 0].reshape(CAP, NW, VOC), (1, 0, 2))
-    rows = jnp.pad(rows, ((0, 0), (0, 0), (0, PADV - VOC)))
-    live = jnp.arange(CAP, dtype=jnp.int32)[None, None, :] < slot_count[:, :, None]
-    coded = slot_request * 16 + jnp.where(live, slot_code, 0)
-    code = lax.dynamic_index_in_dim(coded, n, 1, False).reshape(1, SLOTS)
     dma = pltpu.SemaphoreType.DMA
     vmem = pl.BlockSpec(memory_space=pltpu.VMEM)
     out = pl.pallas_call(
         head_kernel,
         name="head",
         out_shape=jax.ShapeDtypeStruct((VOC, ROWS), f32),
-        in_specs=[vmem] * 5,
+        in_specs=[vmem] * 7,
         out_specs=vmem,
         scratch_shapes=[
             pltpu.VMEM((NW, REQ, D // NN), bf16),
+            pltpu.VMEM((NX, NZ, CAP, PADV), bf16),
+            pltpu.VMEM((NX, NZ, CAP, PADV), bf16),
             pltpu.VMEM((NW, CAP, PADV), bf16),
             pltpu.VMEM((PADV, SLOTS), bf16),
             pltpu.VMEM((NN, VOC, ROWS), f32),
@@ -284,11 +362,19 @@
             pltpu.VMEM((NN, REQ, 128), f32),
             pltpu.VMEM((NX, 8, ROWS), f32),
             pltpu.VMEM((NZ, 8, ROWS), f32),
-            dma((NN,)), dma((NN,)), dma, dma, dma, dma((2, 9)), dma, dma((2, 16)), dma, dma((2, 16)),
+            dma((NN,)), dma((NN,)), dma((NX,)), dma((NX,)), dma, dma, dma, dma((2, 9)), dma, dma((2, 16)), dma, dma((2, 16)),
             dma((NY,)), dma((NY,)), dma((4,)), dma((4,)), dma((NX,)), dma((NX,)), dma((NZ,)), dma((NZ,)),
         ],
-        compiler_params=pltpu.CompilerParams(has_side_effects=True, vmem_limit_bytes=40 << 20),
-    )(hidden, norm_gain[None, :], head_weight.T, rows, code)
+        compiler_params=pltpu.CompilerParams(has_side_effects=True, collective_id=0, vmem_limit_bytes=40 << 20),
+    )(
+        hidden,
+        norm_gain[None, :],
+        head_weight.T,
+        diff_rows[0, 0],
+        jnp.transpose(slot_request, (1, 2, 0)),
+        jnp.transpose(slot_code, (1, 2, 0)),
+        slot_count.T,
+    )
     return out.T
 
 

time: 131 us -> 113 us (0.86)
  the two profiles are of different devices: /device:TPU:8 before, /device:TPU:1 now
where the time goes in v2:
time: 113 us; the launch traced here: 112 us
  Pallas kernels  106 us (94%)
  local copies, waits for them, and re-layouts  6.1 us (5%)
    pallas_call x1, Pallas kernels, body(): pl.pallas_call(head_kernel, name='head', out_shape=jax.ShapeDtypeStruct((...  106 us
    unnamed x15, local copies, waits for them, and re-layouts  6.1 us

profile of v2, /device:TPU:1, one launch (start us, length us, event | category | flops | bytes accessed | tf_op | source)
XLA Modules:
  0.0 112.1 jit_solution(15033065949360808845)
XLA Ops:
  0.0 0.0 copy-start.6
  0.0 0.0 copy-start.5
  0.0 0.7 copy-done.6
  0.7 0.0 copy-done.5
  0.7 0.0 copy-start
  0.7 1.2 %copy-done = bf16[1024,500]{0,1:T(8,128)(2,1)S(1)} copy-done((bf16[1024,500]{0,1:T(8,128)(2,1)S(1)}, bf16[1024,500]{0,1:T(8,128)(2,1)}, u32[]{:S(2)}) %copy-start) | copy-done | bytes 1024024
  1.9 0.0 copy-start.1
  1.9 1.0 copy-done.1
  3.0 0.0 copy-start.2
  3.0 0.8 copy-done.2
  3.8 0.0 copy-start.3
  3.8 0.8 copy-done.3
  4.6 0.0 copy-start.4
  4.6 0.8 copy-done.4
  5.3 106.0 %head.1 = f32[500,256]{1,0:T(8,128)S(1)} custom-call(bf16[32,1024]{1,0:T(8,128)(2,1)S(1)} %copy-done.2, f32[1,1024]{1,0:T(1,128)S(1)} %bitcast.12, bf16[500,1024]{1,0:T(8,128)(2,1)S(1)} %bitcast.8, bf16[8,32000]{1,0:T(8,128)(2,1)S(1)} %bitcast.9, s32[8,8,64]{2,1,0:T(8,128)S(1)} %bitcast.10, s32[8,8,64]{2,1,0:T(8,128)S(1)} %bitcast.11, s32[8,64]{1,0:T(8,128)S(1)} %bitcast.13), custom_call_target="tpu_custom_call" | custom-call | tf_op jit(solution)/shard_map/head/pallas_call | solution.py:346
  111.3 0.8 copy.9
Async XLA Ops:
  0.0 0.7 copy-start.6
  0.0 0.7 copy-start.5
  0.7 1.2 %copy-start = (bf16[1024,500]{0,1:T(8,128)(2,1)S(1)}, bf16[1024,500]{0,1:T(8,128)(2,1)}, u32[]{:S(2)}) copy-start(bf16[1024,500]{0,1:T(8,128)(2,1)} %param.9) | copy-start | bytes 3072004
  1.9 1.0 copy-start.1
  3.0 0.8 copy-start.2
  3.8 0.8 copy-start.3
  4.6 0.8 copy-start.4

commit v3 on v2

--- a/solution.py
+++ b/solution.py
@@ -67,7 +67,9 @@
     relay[x] = bundle[x]
 
     values = h_ref[...].astype(f32)
-    sq[n] = jnp.broadcast_to(jnp.sum(values * values, axis=1, keepdims=True), (REQ, 128))
+    diagonal = lax.broadcasted_iota(jnp.int32, (REQ, 128), 0) == lax.broadcasted_iota(jnp.int32, (REQ, 128), 1)
+    squares = jnp.broadcast_to(jnp.sum(values * values, axis=1, keepdims=True), (REQ, 128))
+    sq[n] = jnp.sum(jnp.where(diagonal, squares, 0.0), axis=0, keepdims=True)
 
     pl.semaphore_wait(barrier, NN + NX + NZ - 3)
 
@@ -94,10 +96,11 @@
             relay.at[source].at[(z + k) % NZ], recv_rows.at[row], a2a_send, a2a_recv, wide_of(k, 0), n
         )
 
-    def relay_start(k):
+    def relay_start(k, first=0, last=NZ - 1):
         source = (x - k + NX) % NX
-        recv_rows[z * NX + source] = relay[source, z]
-        for far in FAR:
+        if first == 0:
+            recv_rows[z * NX + source] = relay[source, z]
+        for far in FAR[first:last]:
             relay_copy(source, far).start()
 
     for k in (2, 1, 3):
@@ -123,7 +126,8 @@
 
     for k in range(1, NN):
         sq_arrival(k).wait_recv()
-    total = jnp.sum(sq[...], axis=0)[:, :1]
+    total = jnp.broadcast_to(jnp.sum(sq[...], axis=0), (REQ, 128))
+    total = jnp.sum(jnp.where(diagonal, total, 0.0), axis=1, keepdims=True)
     scales = lax.rsqrt(total / D + EPS)
     act[w] = (values * scales * g_ref[...]).astype(bf16)
 
@@ -189,6 +193,62 @@
         requested = lax.broadcasted_iota(jnp.int32, (ROWS, SLOTS), 0) + block * ROWS
         chosen = jnp.where(requests == requested.astype(f32), quarters, 0.0).astype(bf16)
         part[block] += lax.dot_general(rows_t[pl.ds(0, VOC)], chosen, NT, preferred_element_type=f32)
+
+    def take_rows():
+        pltpu.make_async_copy(recv_rows.at[pl.ds(0, 60)], recv_rows.at[pl.ds(0, 60)], a2a_recv).wait()
+        rows_t[...] = jnp.transpose(recv_rows[...].reshape(SLOTS, PADV))
+
+    def north(k):
+        return ((y + k + NY) % NY) * NC + c
+
+    def away_of(block):
+        return (block // NC - y + NY) % NY
+
+    def pair_copy(block):
+        r = away_of(block)
+        return remote(part.at[block], pair.at[r], p_send.at[r], p_recv.at[r], w, y * NC + 1 - c)
+
+    lanes = (pl.ds(0, ROWS // 2), pl.ds(ROWS // 2, ROWS // 2))
+
+    def half_copy(side, block):
+        step = 1 if side == 0 else -1
+        return remote(part.at[block].at[:, lanes[side]], half.at[side], y_send.at[side], y_recv.at[side], w, north(step))
+
+    def full_copy(side, block):
+        step = 1 if side == 0 else -1
+        return remote(part.at[block], full.at[side], y_send.at[2 + side], y_recv.at[2 + side], w, north(step))
+
+    def across_cores(d):
+        block = block_of(d)
+
+        @pl.when(block % NC != c)
+        def _():
+            pair_copy(block).start()
+
+    def from_core(d):
+        block = block_of(d)
+        r = away_of(block)
+
+        @pl.when(block % NC == c)
+        def _():
+            pair_copy(block).wait_recv()
+            part[block] += pair[r]
+
+        @pl.when((block % NC == c) & (r == 2))
+        def _():
+            half_copy(0, block).start()
+            half_copy(1, block).start()
+
+    def to_owner(d):
+        block = block_of(d)
+        r = away_of(block)
+        for side in range(2):
+
+            @pl.when((block % NC == c) & (r == (1, 3)[side]))
+            def _():
+                half_copy(side, block).wait_recv()
+                part[block, :, lanes[side]] += half[side]
+                full_copy(side, block).start()
 
     for d in range(9):
         if d in range(1, 8):
@@ -206,96 +266,79 @@
         for q, dz in events[d]:
             for side in range(2):
                 x_copy(side, q, dz).start()
-        if d < 3:
-            k = (1, 3, 2)[d]
-            bundle_arrival(k).wait_recv()
-            relay_start(k)
+        if d == 0:
+            bundle_arrival(1).wait_recv()
+            relay_start(1, 0, 8)
+        if d == 1:
+            relay_start(1, 8, 15)
+        if d == 2:
+            bundle_arrival(3).wait_recv()
+            relay_start(3, 0, 8)
+        if d == 3:
+            relay_start(3, 8, 15)
+        if d == 4:
+            bundle_arrival(2).wait_recv()
+            relay_start(2, 0, 8)
+        if d == 5:
+            relay_start(2, 8, 15)
         if d >= 1:
             forward_x(d - 1)
         if d >= 2:
             last_x(d - 2)
         if d >= 3:
             product(d - 2)
+        if d == 7:
+            take_rows()
     forward_x(8)
-
-    pltpu.make_async_copy(recv_rows.at[pl.ds(0, 60)], recv_rows.at[pl.ds(0, 60)], a2a_recv).wait()
-    rows_t[...] = jnp.transpose(recv_rows[...].reshape(SLOTS, PADV))
-
-    def north(k):
-        return ((y + k + NY) % NY) * NC + c
-
-    def away_of(block):
-        return (block // NC - y + NY) % NY
-
-    def pair_copy(block):
-        r = away_of(block)
-        return remote(part.at[block], pair.at[r], p_send.at[r], p_recv.at[r], w, y * NC + 1 - c)
-
-    lanes = (pl.ds(0, ROWS // 2), pl.ds(ROWS // 2, ROWS // 2))
-
-    def half_copy(side, block):
-        step = 1 if side == 0 else -1
-        return remote(part.at[block].at[:, lanes[side]], half.at[side], y_send.at[side], y_recv.at[side], w, north(step))
-
-    def full_copy(side, block):
-        step = 1 if side == 0 else -1
-        return remote(part.at[block], full.at[side], y_send.at[2 + side], y_recv.at[2 + side], w, north(step))
-
-    def across_cores(d):
-        block = block_of(d)
-
-        @pl.when(block % NC != c)
-        def _():
-            pair_copy(block).start()
-
-    def from_core(d):
-        block = block_of(d)
-        r = away_of(block)
-
-        @pl.when(block % NC == c)
-        def _():
-            pair_copy(block).wait_recv()
-            part[block] += pair[r]
-
-        @pl.when((block % NC == c) & (r == 2))
-        def _():
-            half_copy(0, block).start()
-            half_copy(1, block).start()
-
-    def to_owner(d):
-        block = block_of(d)
-        r = away_of(block)
-        for side in range(2):
-
-            @pl.when((block % NC == c) & (r == (1, 3)[side]))
-            def _():
-                half_copy(side, block).wait_recv()
-                part[block, :, lanes[side]] += half[side]
-                full_copy(side, block).start()
-
-    for d in range(1, 17):
-        if d in (7, 8):
-            last_x(d)
-            product(d)
-        if d <= 8:
-            add_rows(d)
-            across_cores(d)
-        if 1 <= d - 3 <= 8:
-            from_core(d - 3)
-        if 1 <= d - 8 <= 8:
-            to_owner(d - 8)
+    add_rows(1)
+    across_cores(1)
+    add_rows(2)
+    across_cores(2)
+    add_rows(3)
+    across_cores(3)
+    add_rows(4)
+    across_cores(4)
+    add_rows(5)
+    across_cores(5)
+    add_rows(6)
+    across_cores(6)
+    from_core(1)
+    from_core(2)
+    from_core(3)
+    from_core(4)
+    from_core(5)
+    from_core(6)
+    last_x(7)
+    product(7)
+    add_rows(7)
+    across_cores(7)
+    last_x(8)
+    product(8)
+    add_rows(8)
+    across_cores(8)
+    from_core(7)
+    from_core(8)
+    to_owner(1)
+    to_owner(2)
+    to_owner(3)
+    to_owner(4)
+    to_owner(5)
+    to_owner(6)
+    to_owner(7)
+    to_owner(8)
+
     for side in range(2):
         full_copy(side, n).wait_recv()
     logits = part[n] + full[0] + full[1]
 
     def merged(buffer):
-        peaks, masses = buffer[:, 0:1, :], buffer[:, 4:5, :]
+        peaks, masses = buffer[:, 0:1, :], buffer[:, 1:2, :]
         peak = jnp.max(peaks, axis=0)
         return peak, jnp.sum(masses * jnp.exp(peaks - peak[None]), axis=0)
 
     def put(buffer, index, peak, mass):
-        buffer[index, 0:4, :] = jnp.broadcast_to(peak, (4, ROWS))
-        buffer[index, 4:8, :] = jnp.broadcast_to(mass, (4, ROWS))
+        buffer[index, 0:1, :] = peak
+        buffer[index, 1:2, :] = mass
 
     peak = jnp.max(logits, axis=0, keepdims=True)
     mass = jnp.sum(jnp.exp(logits - peak), axis=0, keepdims=True)
@@ -359,9 +402,9 @@
             pltpu.VMEM((NY, VOC, ROWS), f32),
             pltpu.VMEM((2, VOC, ROWS // 2), f32),
             pltpu.VMEM((2, VOC, ROWS), f32),
-            pltpu.VMEM((NN, REQ, 128), f32),
-            pltpu.VMEM((NX, 8, ROWS), f32),
-            pltpu.VMEM((NZ, 8, ROWS), f32),
+            pltpu.VMEM((NN, 1, 128), f32),
+            pltpu.VMEM((NX, 2, ROWS), f32),
+            pltpu.VMEM((NZ, 2, ROWS), f32),
             dma((NN,)), dma((NN,)), dma((NX,)), dma((NX,)), dma, dma, dma, dma((2, 9)), dma, dma((2, 16)), dma, dma((2, 16)),
             dma((NY,)), dma((NY,)), dma((4,)), dma((4,)), dma((NX,)), dma((NX,)), dma((NZ,)), dma((NZ,)),
         ],

time: 113 us -> 109 us (0.965)
  the two profiles are of different devices: /device:TPU:1 before, /device:TPU:32 now
where the time goes in v3:
time: 109 us; the launch traced here: 108 us
  Pallas kernels  102 us (94%)
  local copies, waits for them, and re-layouts  6.1 us (6%)
    pallas_call x1, Pallas kernels, body(): pl.pallas_call(head_kernel, name='head', out_shape=jax.ShapeDtypeStruct((...  102 us
    unnamed x15, local copies, waits for them, and re-layouts  6.1 us

profile of v3, /device:TPU:32, one launch (start us, length us, event | category | flops | bytes accessed | tf_op | source)
XLA Modules:
  0.0 108.0 jit_solution(8053844357648806493)
XLA Ops:
  0.0 0.0 copy-start.6
  0.0 0.0 copy-start.5
  0.0 0.7 copy-done.6
  0.7 0.0 copy-done.5
  0.7 0.0 copy-start
  0.7 1.2 %copy-done = bf16[1024,500]{0,1:T(8,128)(2,1)S(1)} copy-done((bf16[1024,500]{0,1:T(8,128)(2,1)S(1)}, bf16[1024,500]{0,1:T(8,128)(2,1)}, u32[]{:S(2)}) %copy-start) | copy-done | bytes 1024024
  1.9 0.0 copy-start.1
  1.9 1.0 copy-done.1
  3.0 0.0 copy-start.2
  3.0 0.8 copy-done.2
  3.8 0.0 copy-start.3
  3.8 0.8 copy-done.3
  4.6 0.0 copy-start.4
  4.6 0.8 copy-done.4
  5.3 101.8 %head.1 = f32[500,256]{1,0:T(8,128)S(1)} custom-call(bf16[32,1024]{1,0:T(8,128)(2,1)S(1)} %copy-done.2, f32[1,1024]{1,0:T(1,128)S(1)} %bitcast.12, bf16[500,1024]{1,0:T(8,128)(2,1)S(1)} %bitcast.8, bf16[8,32000]{1,0:T(8,128)(2,1)S(1)} %bitcast.9, s32[8,8,64]{2,1,0:T(8,128)S(1)} %bitcast.10, s32[8,8,64]{2,1,0:T(8,128)S(1)} %bitcast.11, s32[8,64]{1,0:T(8,128)S(1)} %bitcast.13), custom_call_target="tpu_custom_call" | custom-call | tf_op jit(solution)/shard_map/head/pallas_call | solution.py:389
  107.2 0.8 copy.9
Async XLA Ops:
  0.0 0.7 copy-start.6
  0.0 0.7 copy-start.5
  0.7 1.2 %copy-start = (bf16[1024,500]{0,1:T(8,128)(2,1)S(1)}, bf16[1024,500]{0,1:T(8,128)(2,1)}, u32[]{:S(2)}) copy-start(bf16[1024,500]{0,1:T(8,128)(2,1)} %param.9) | copy-start | bytes 3072004
  1.9 1.0 copy-start.1
  3.0 0.8 copy-start.2
  3.8 0.8 copy-start.3
  4.6 0.8 copy-start.4

commit v4 on v3

--- a/solution.py
+++ b/solution.py
@@ -251,35 +251,42 @@
                 full_copy(side, block).start()
 
     for d in range(9):
-        if d in range(1, 8):
+        for side in range(2 if d < 7 else 0):
+            if d > 0:
+                z_arrival(side, d).wait_recv()
+            z_copy(side, d).start()
+            if d > 0:
+                q, dz = events[d][side]
+                x_copy(0, q, dz).start()
+                x_copy(1, q, dz).start()
+        if d == 7:
             for side in range(2):
                 z_arrival(side, d).wait_recv()
         if d == 8:
             z_arrival(0, 8, top).wait_recv()
             z_arrival(1, 8, bottom).wait_recv()
-        if d < 7:
-            for side in range(2):
-                z_copy(side, d).start()
         if d == 7:
             z_copy(0, 7, top).start()
             z_copy(1, 7, bottom).start()
-        for q, dz in events[d]:
+        for q, dz in events[d] if d in (0, 7, 8) else ():
             for side in range(2):
                 x_copy(side, q, dz).start()
         if d == 0:
             bundle_arrival(1).wait_recv()
-            relay_start(1, 0, 8)
+            relay_start(1, 0, 5)
         if d == 1:
-            relay_start(1, 8, 15)
+            relay_start(1, 5, 10)
         if d == 2:
+            relay_start(1, 10, 15)
+        if d == 3:
             bundle_arrival(3).wait_recv()
             relay_start(3, 0, 8)
-        if d == 3:
+        if d == 4:
             relay_start(3, 8, 15)
-        if d == 4:
+        if d == 5:
             bundle_arrival(2).wait_recv()
             relay_start(2, 0, 8)
-        if d == 5:
+        if d == 6:
             relay_start(2, 8, 15)
         if d >= 1:
             forward_x(d - 1)

time: 109 us -> 106 us (0.972)
  Pallas kernels: 102 us -> 99.3 us
    pallas_call x1, Pallas kernels: 102 us -> 99.3 us  [body(): pl.pallas_call(head_kernel, name='head', out_shape=jax.ShapeDtypeStruct((...]
where the time goes in v4:
time: 106 us; the launch traced here: 105 us
  Pallas kernels  99.3 us (94%)
  local copies, waits for them, and re-layouts  6.1 us (6%)
    pallas_call x1, Pallas kernels, body(): pl.pallas_call(head_kernel, name='head', out_shape=jax.ShapeDtypeStruct((...  99.3 us
    unnamed x15, local copies, waits for them, and re-layouts  6.1 us

profile of v4, /device:TPU:32, one launch (start us, length us, event | category | flops | bytes accessed | tf_op | source)
XLA Modules:
  0.0 105.4 jit_solution(9352339050453898908)
XLA Ops:
  0.0 0.0 copy-start.6
  0.0 0.0 copy-start.5
  0.0 0.7 copy-done.6
  0.7 0.0 copy-done.5
  0.7 0.0 copy-start
  0.7 1.2 %copy-done = bf16[1024,500]{0,1:T(8,128)(2,1)S(1)} copy-done((bf16[1024,500]{0,1:T(8,128)(2,1)S(1)}, bf16[1024,500]{0,1:T(8,128)(2,1)}, u32[]{:S(2)}) %copy-start) | copy-done | bytes 1024024
  1.9 0.0 copy-start.1
  1.9 1.0 copy-done.1
  3.0 0.0 copy-start.2
  3.0 0.8 copy-done.2
  3.8 0.0 copy-start.3
  3.8 0.8 copy-done.3
  4.6 0.0 copy-start.4
  4.6 0.8 copy-done.4
  5.3 99.3 %head.1 = f32[500,256]{1,0:T(8,128)S(1)} custom-call(bf16[32,1024]{1,0:T(8,128)(2,1)S(1)} %copy-done.2, f32[1,1024]{1,0:T(1,128)S(1)} %bitcast.12, bf16[500,1024]{1,0:T(8,128)(2,1)S(1)} %bitcast.8, bf16[8,32000]{1,0:T(8,128)(2,1)S(1)} %bitcast.9, s32[8,8,64]{2,1,0:T(8,128)S(1)} %bitcast.10, s32[8,8,64]{2,1,0:T(8,128)S(1)} %bitcast.11, s32[8,64]{1,0:T(8,128)S(1)} %bitcast.13), custom_call_target="tpu_custom_call" | custom-call | tf_op jit(solution)/shard_map/head/pallas_call | solution.py:396
  104.6 0.8 copy.9
Async XLA Ops:
  0.0 0.7 copy-start.6
  0.0 0.7 copy-start.5
  0.7 1.2 %copy-start = (bf16[1024,500]{0,1:T(8,128)(2,1)S(1)}, bf16[1024,500]{0,1:T(8,128)(2,1)}, u32[]{:S(2)}) copy-start(bf16[1024,500]{0,1:T(8,128)(2,1)} %param.9) | copy-start | bytes 3072004
  1.9 1.0 copy-start.1
  3.0 0.8 copy-start.2
  3.8 0.8 copy-start.3
  4.6 0.8 copy-start.4

commit v5 on v4

--- a/solution.py
+++ b/solution.py
@@ -55,12 +55,12 @@
             barrier, inc=1, device_id={"wide": wide, "narrow": narrow}, device_id_type=pl.DeviceIdType.MESH
         )
 
-    for k in range(1, NN):
+    for k in FAR:
+        greet(wide_of(k, 0), n)
+    for k in (4, 5, 3, 2, 6, 1, 7):
         greet(w, (n + k) % NN)
-    for k in range(1, NX):
+    for k in (2, 1, 3):
         greet(wide_of(0, k), n)
-    for k in range(1, NZ):
-        greet(wide_of(k, 0), n)
 
     for target in range(NW):
         bundle[target % NX, target // NX, :, 0:VOC] = diff_ref[:, target * VOC : (target + 1) * VOC]
@@ -80,7 +80,7 @@
         peer = (n - k + NN) % NN
         return remote(sq.at[peer], sq.at[peer], sq_send.at[k], sq_recv.at[k], w, peer)
 
-    for k in range(1, NN):
+    for k in (4, 5, 3, 2, 6, 1, 7):
         sq_copy(k).start()
 
     def bundle_copy(k):

time: 106 us -> 106 us (level)
  no operation moved by 1% of the time
where the time goes in v5:
time: 106 us
  Pallas kernels  99.5 us (94%)
  local copies, waits for them, and re-layouts  6.1 us (6%)
    pallas_call x1, Pallas kernels, body(): pl.pallas_call(head_kernel, name='head', out_shape=jax.ShapeDtypeStruct((...  99.5 us
    unnamed x15, local copies, waits for them, and re-layouts  6.1 us

profile of v5, /device:TPU:32, one launch (start us, length us, event | category | flops | bytes accessed | tf_op | source)
XLA Modules:
  0.0 105.6 jit_solution(4801933162811309852)
XLA Ops:
  0.0 0.0 copy-start.6
  0.0 0.0 copy-start.5
  0.0 0.7 copy-done.6
  0.7 0.0 copy-done.5
  0.7 0.0 copy-start
  0.7 1.2 %copy-done = bf16[1024,500]{0,1:T(8,128)(2,1)S(1)} copy-done((bf16[1024,500]{0,1:T(8,128)(2,1)S(1)}, bf16[1024,500]{0,1:T(8,128)(2,1)}, u32[]{:S(2)}) %copy-start) | copy-done | bytes 1024024
  1.9 0.0 copy-start.1
  1.9 1.0 copy-done.1
  3.0 0.0 copy-start.2
  3.0 0.8 copy-done.2
  3.8 0.0 copy-start.3
  3.8 0.8 copy-done.3
  4.6 0.0 copy-start.4
  4.6 0.8 copy-done.4
  5.3 99.5 %head.1 = f32[500,256]{1,0:T(8,128)S(1)} custom-call(bf16[32,1024]{1,0:T(8,128)(2,1)S(1)} %copy-done.2, f32[1,1024]{1,0:T(1,128)S(1)} %bitcast.12, bf16[500,1024]{1,0:T(8,128)(2,1)S(1)} %bitcast.8, bf16[8,32000]{1,0:T(8,128)(2,1)S(1)} %bitcast.9, s32[8,8,64]{2,1,0:T(8,128)S(1)} %bitcast.10, s32[8,8,64]{2,1,0:T(8,128)S(1)} %bitcast.11, s32[8,64]{1,0:T(8,128)S(1)} %bitcast.13), custom_call_target="tpu_custom_call" | custom-call | tf_op jit(solution)/shard_map/head/pallas_call | solution.py:396
  104.8 0.8 copy.9
Async XLA Ops:
  0.0 0.7 copy-start.6
  0.0 0.7 copy-start.5
  0.7 1.2 %copy-start = (bf16[1024,500]{0,1:T(8,128)(2,1)S(1)}, bf16[1024,500]{0,1:T(8,128)(2,1)}, u32[]{:S(2)}) copy-start(bf16[1024,500]{0,1:T(8,128)(2,1)} %param.9) | copy-start | bytes 3072004
  1.9 1.0 copy-start.1
  3.0 0.8 copy-start.2
  3.8 0.8 copy-start.3
  4.6 0.8 copy-start.4
